TPU v7x, 32 devices: a whole 2x2x4 slice. The times are simulated.
32 devices in a mesh: gx: 4 (over x, core), gy: 2 (over y), gz: 4 (over z).
Axes of the slice: x: 2, y: 2, z: 4, core: 2. Of those that a mesh axis runs over, the one named last changes fastest.
Arguments:
- state: float32 [24, 32, 16, 512], P(None, 'gx', 'gy', 'gz'), may hold values from -6 to 6
- coarse_bricks: float32 [4, 2, 4, 235008], P('gx', 'gy', 'gz'), may hold values from -6 to 6
- shifts: int32 [2], replicated, may hold values from 1 to 8, as said below
- brick_owner: int32 [4], replicated, may hold values from 0 to 3, each once
Outputs:
- new_state: float32 [24, 32, 16, 512], P(None, 'gx', 'gy', 'gz')
Inputs may be any that keep to these rules, and one draw needn't show every extreme that they name: shifts[0] and shifts[1] are each from 1 to 8, and at least one of them equals 8. `brick_owner`: a permutation of the gx indices.
All inputs are finite; a program needn't handle non-finite values.
Results may differ from a plain program's by a relative error of at most 0.000062.
Values sent between devices are 32-bit elements; how exact they have to be, the bound alone decides.
A program may use at most 128 MiB of HBM per device.

v0:
```python
import jax
import jax.numpy as jnp
from jax import lax
from jax.experimental import pallas as pl
from jax.experimental.pallas import tpu as pltpu
from jax.sharding import PartitionSpec as P

EVEN_W = (-0.0390625, 0.2734375, 0.8203125, -0.0546875)
ODD_W = (-0.0546875, 0.8203125, 0.2734375, -0.0390625)
PAIRS = ((0, 0), (0, 1), (0, 2), (1, 1), (1, 2), (2, 2))
SIGMA = 0.3
DRIVER_DAMP = 2.0
STEP = 0.25
HIGH = lax.Precision.HIGHEST


def passed_along(block, axis, distance):
    devices = range(lax.axis_size(axis))
    route = [(i - distance, i) for i in devices if i - distance in devices]
    return lax.ppermute(block, axis, route)


MESH = pl.DeviceIdType.MESH
ORDER = (0, 17, 18, 19, 20, 1, 2, 3, 4, 5, 6, 7, 8, 9, 10, 11, 12, 13, 14, 15, 16, 21, 22, 23)
PLACE = {field: place for place, field in enumerate(ORDER)}
MIXED = 5
FACES = tuple(
    tuple(side if d == axis else 0 for d in range(3)) for axis in range(3) for side in (-1, 1)
)
EDGES = tuple(
    (dx, dy, dz)
    for dx in (-1, 0, 1)
    for dy in (-1, 0, 1)
    for dz in (-1, 0, 1)
    if abs(dx) + abs(dy) + abs(dz) == 2
)
ROUTES = FACES + EDGES


def slope(m2, m1, p1, p2):
    return (8.0 * (p1 - m1) - (p2 - m2)) * (1.0 / 12.0)


def step_kernel(
    start_ref, out_ref, box, zhalo, acc, slopes, ysend, yrecv, csend, crecv, zsend, zcore, zx, zy,
    send_sem, recv_sem,
):
    fields = start_ref.shape[0]
    groups = zsend.shape[2]
    counts = tuple(lax.axis_size(name) for name in ("gx", "gy", "gz"))
    place = tuple(lax.axis_index(name) for name in ("gx", "gy", "gz"))
    lane = lax.broadcasted_iota(jnp.int32, (8, 128), 1)
    row = lax.broadcasted_iota(jnp.int32, (8, 128), 0)
    zero = jnp.zeros((8, 128), jnp.float32)

    def present(route):
        ok = None
        for d in range(3):
            if route[d] != 0:
                here = place[d] > 0 if route[d] < 0 else place[d] < counts[d] - 1
                ok = here if ok is None else jnp.logical_and(ok, here)
        return ok

    def peer(route):
        return tuple(place[d] + route[d] for d in range(3))

    def opposite(route):
        return tuple(-side for side in route)

    def wipe_field(f, carry):
        for slot in range(2):
            for x in range(14):
                for y in (0, 16) if 3 <= x < 11 else (0, 8, 16):
                    box[slot, f, x, pl.ds(y, 8), :] = zero
        for x in range(8):
            value = start_ref[f, x]
            acc[f, x] = value
        return carry

    lax.fori_loop(0, fields, wipe_field, 0)
    for f in range(fields):
        for x in range(8):
            box[0, f, 3 + x, pl.ds(8, 8), :] = start_ref[ORDER[f], x]
    for slot in range(2):
        for z in range(2):
            for g in range(groups):
                zcore[slot, z, g] = zero
            for side in range(2):
                for g in range(2):
                    zx[slot, side, z, g] = zero
                    zy[slot, side, z, g] = zero
            for side in range(2):
                for f in range(MIXED):
                    crecv[slot, z, side, f] = zero

    def wipe_y(f, carry):
        for slot in range(2):
            for side in range(2):
                for j in range(3):
                    yrecv[slot, side, j, f] = zero
        return carry

    lax.fori_loop(0, fields, wipe_y, 0)

    barrier = pltpu.get_barrier_semaphore()
    total = jnp.int32(0)
    for route in ROUTES:
        ok = present(route)
        total = total + ok.astype(jnp.int32)

        @pl.when(ok)
        def _(route=route):
            pl.semaphore_signal(barrier, inc=1, device_id=peer(route), device_id_type=MESH)

    pl.semaphore_wait(barrier, total)

    def message(number, slot):
        route = ROUTES[number]
        dx, dy, dz = route
        low = lambda side: 1 if side < 0 else 0
        high = lambda side: 0 if side < 0 else 1
        if dx != 0 and dy == 0 and dz == 0:
            source = box.at[slot, :, pl.ds(3 if dx < 0 else 8, 3), pl.ds(8, 8), :]
            target = box.at[slot, :, pl.ds(11 if dx < 0 else 0, 3), pl.ds(8, 8), :]
        elif dy != 0 and dx == 0 and dz == 0:
            source = ysend.at[slot, high(dy)]
            target = yrecv.at[slot, low(dy)]
        elif dz != 0 and dx == 0 and dy == 0:
            source = zsend.at[slot, high(dz)]
            target = zcore.at[slot, low(dz)]
        elif dz == 0:
            source = csend.at[slot, high(dy)]
            target = crecv.at[slot, low(dy), low(dx)]
        elif dy == 0:
            source = zsend.at[slot, high(dz), pl.ds(0, 2)]
            target = zx.at[slot, low(dx), low(dz)]
        else:
            source = zsend.at[slot, high(dz), pl.ds(0, 2)]
            target = zy.at[slot, low(dy), low(dz)]
        return pltpu.make_async_remote_copy(
            src_ref=source,
            dst_ref=target,
            send_sem=send_sem.at[number],
            recv_sem=recv_sem.at[slot, number],
            device_id=peer(route),
            device_id_type=MESH,
        )

    def launch(slot, wanted):
        for number, route in enumerate(ROUTES):
            if wanted(route):

                @pl.when(present(route))
                def _(number=number):
                    message(number, slot).start()

    def unpacked(from_low, from_high, t):
        return jnp.where(
            lane < 64,
            pltpu.roll(from_high, (128 - 4 * t) % 128, axis=1),
            pltpu.roll(from_low, (124 - 4 * t) % 128, axis=1),
        )

    def stage(s, carry):
        slot = lax.rem(s, 2)
        launch(slot, lambda r: r[1] == 0 and r[2] == 0)

        def pack_y(f, c):
            for j in range(3):
                ysend[slot, 0, j, f] = box[slot, f, pl.ds(3, 8), 8 + j, :]
                ysend[slot, 1, j, f] = box[slot, f, pl.ds(3, 8), 13 + j, :]
            return c

        lax.fori_loop(0, fields, pack_y, 0)
        launch(slot, lambda r: r[0] == 0 and r[2] == 0)
        outer = jnp.logical_or(row < 2, row >= 6)
        for side in range(2):
            for f in range(MIXED):
                csend[slot, side, f] = jnp.where(
                    outer,
                    ysend[slot, side, side, f],
                    pltpu.roll(ysend[slot, side, side + 1, f], 4, axis=0),
                )
        launch(slot, lambda r: r[2] == 0 and r[0] != 0 and r[1] != 0)

        def pack_z(g, c):
            low = zero
            high = zero
            for q in range(4):
                for x in range(8):
                    t = q * 8 + x
                    value = box[slot, 4 * g + q, 3 + x, pl.ds(8, 8), :]
                    inside = jnp.logical_and(lane >= 4 * t, lane < 4 * t + 4)
                    low = jnp.where(inside, pltpu.roll(value, 4 * t, axis=1), low)
                    high = jnp.where(inside, pltpu.roll(value, (4 * t + 4) % 128, axis=1), high)
            zsend[slot, 0, g] = low
            zsend[slot, 1, g] = high
            return c

        lax.fori_loop(0, groups, pack_z, 0)
        launch(slot, lambda r: r[2] != 0)

        for number, route in enumerate(ROUTES):

            @pl.when(present(opposite(route)))
            def _(number=number):
                message(number, slot).wait_recv()

        def spread_y(f, c):
            for j in range(3):
                box[slot, f, pl.ds(3, 8), 5 + j, :] = yrecv[slot, 0, j, f]
                box[slot, f, pl.ds(3, 8), 16 + j, :] = yrecv[slot, 1, j, f]
            return c

        lax.fori_loop(0, fields, spread_y, 0)
        for f in range(MIXED):
            for side, first_row in ((0, 6), (1, 16)):
                for j in range(2):
                    box[slot, f, pl.ds(1, 2), first_row + j, :] = crecv[
                        slot, side, 0, f, pl.ds(6 if j == 0 else 2, 2), :
                    ]
                    box[slot, f, pl.ds(11, 2), first_row + j, :] = crecv[
                        slot, side, 1, f, pl.ds(0 if j == 0 else 4, 2), :
                    ]

        def spread_z(g, c):
            from_low = zcore[slot, 0, g]
            from_high = zcore[slot, 1, g]
            for q in range(4):
                for x in range(8):
                    zhalo[4 * g + q, 2 + x, pl.ds(8, 8), :] = unpacked(
                        from_low, from_high, q * 8 + x
                    )
            return c

        lax.fori_loop(0, groups, spread_z, 0)
        for f in range(MIXED):
            g, q = f // 4, f % 4
            for side in range(2):
                low_x, high_x = zx[slot, side, 0, g], zx[slot, side, 1, g]
                for k in range(2):
                    x = 6 + k if side == 0 else k
                    at = k if side == 0 else 10 + k
                    zhalo[f, at, pl.ds(8, 8), :] = unpacked(low_x, high_x, q * 8 + x)
                low_y, high_y = zy[slot, side, 0, g], zy[slot, side, 1, g]
                for x in range(8):
                    zhalo[f, 2 + x, pl.ds(16 * side, 8), :] = unpacked(low_y, high_y, q * 8 + x)

        share = jnp.where(jnp.logical_or(s == 0, s == 3), STEP / 6.0, STEP / 3.0)
        share = share.astype(jnp.float32)
        reach = jnp.where(s == 2, STEP, 0.5 * STEP).astype(jnp.float32)
        later = 1 - slot

        def slab(x, c):
            def at_z(value, halo, amount):
                if amount > 0:
                    return pltpu.roll(jnp.where(lane < amount, halo, value), 128 - amount, axis=1)
                return pltpu.roll(
                    jnp.where(lane >= 128 + amount, halo, value), -amount, axis=1
                )

            def tile(f, dx=0, dy=0):
                return box[slot, f, 3 + x + dx, pl.ds(8 + dy, 8), :]

            def slope_z(value, halo):
                return slope(*(at_z(value, halo, amount) for amount in (-2, -1, 1, 2)))

            def study(name, gradient=False):
                f = PLACE[name]
                centre = tile(f)
                halo = zhalo[f, 2 + x, pl.ds(8, 8), :]
                pairs = []
                grads = []
                for d in range(3):
                    cells = {}
                    for amount in (-3, -2, -1, 1, 2, 3):
                        if d == 0:
                            cells[amount] = tile(f, amount, 0)
                        elif d == 1:
                            cells[amount] = tile(f, 0, amount)
                        else:
                            cells[amount] = at_z(centre, halo, amount)
                    pairs.append([cells[k] + cells[-k] for k in (1, 2, 3)])
                    if gradient:
                        grads.append(slope(cells[-2], cells[-1], cells[1], cells[2]))
                ones, twos, threes = [pairs[0][k] + pairs[1][k] + pairs[2][k] for k in range(3)]
                damp = (threes - 6.0 * twos + 15.0 * ones - 60.0 * centre) * (SIGMA / 64.0)
                lap = (16.0 * ones - twos - 90.0 * centre) * (1.0 / 12.0)
                curves = [
                    (16.0 * pairs[d][0] - pairs[d][1] - 30.0 * centre) * (1.0 / 12.0)
                    for d in range(3)
                ]
                return centre, damp, lap, curves, grads

            def finish(name, rate):
                f = PLACE[name]
                total = acc[name, x] + share * rate
                acc[name, x] = total
                box[later, f, 3 + x, pl.ds(8, 8), :] = start_ref[name, x] + reach * rate

            def across_x(name, y):
                f = PLACE[name]
                return slope(
                    *(box[slot, f, 3 + x + k, pl.ds(y, 8), :] for k in (-2, -1, 1, 2))
                )

            def halo_x(name):
                f = PLACE[name]
                return slope(
                    *(zhalo[f, 2 + x + k, pl.ds(8, 8), :] for k in (-2, -1, 1, 2))
                )

            def along_y(name):
                f = PLACE[name]
                return slope(*(tile(f, 0, k) for k in (-2, -1, 1, 2)))

            def halo_y(name):
                f = PLACE[name]
                return slope(
                    *(zhalo[f, 2 + x, pl.ds(8 + k, 8), :] for k in (-2, -1, 1, 2))
                )

            def mixed_xy(number, value):
                for y in (0, 8, 16):
                    slopes[number, pl.ds(y, 8), :] = value(lambda name: across_x(name, y))
                return slope(*(slopes[number, pl.ds(8 + k, 8), :] for k in (-2, -1, 1, 2)))

            def mixed_xz(value):
                return slope_z(value(lambda name: across_x(name, 8)), value(halo_x))

            def mixed_yz(value):
                return slope_z(value(along_y), value(halo_y))

            both = lambda part: part(17) + 2.0 * part(0)
            only = lambda name: (lambda part: part(name))

            curv, curv_damp, _, _, curv_grad = study(7, True)
            phi, phi_damp, _, phi_curves, _ = study(0)
            lapse, lapse_damp, lapse_lap, lapse_curves, _ = study(17)
            finish(17, lapse_damp - 2.0 * curv)
            finish(7, curv_damp - lapse_lap)
            shift_parts = [study(18 + i, True) for i in range(3)]
            shift_grad = [[shift_parts[j][4][d] for j in range(3)] for d in range(3)]
            spread = shift_grad[0][0] + shift_grad[1][1] + shift_grad[2][2]
            finish(0, phi_damp + (spread - curv) * (1.0 / 6.0))
            crossed = (
                mixed_xy(0, only(19)) + mixed_xz(only(20)),
                mixed_xy(1, only(18)) + mixed_yz(only(20)),
                mixed_xz(only(18)) + mixed_yz(only(19)),
            )
            gamma_grad = []
            gamma_parts = [study(14 + i, True) for i in range(3)]
            gamma_grad = [[gamma_parts[j][4][d] for j in range(3)] for d in range(3)]
            for i in range(3):
                rate = (
                    shift_parts[i][2]
                    - (4.0 / 3.0) * curv_grad[i]
                    + (shift_parts[i][3][i] + crossed[i]) * (1.0 / 3.0)
                )
                finish(14 + i, rate + gamma_parts[i][1])
                driver, driver_damp, _, _, _ = study(21 + i)
                finish(18 + i, shift_parts[i][1] + 0.75 * driver)
                finish(21 + i, driver_damp + rate - DRIVER_DAMP * driver)
            hessian = {
                (0, 1): mixed_xy(2, both),
                (0, 2): mixed_xz(both),
                (1, 2): mixed_yz(both),
            }
            for i in range(3):
                hessian[(i, i)] = lapse_curves[i] + 2.0 * phi_curves[i]
            ricci = []
            free_damp = []
            for n, (i, j) in enumerate(PAIRS):
                free, damp, _, _, _ = study(8 + n)
                free_damp.append(damp)
                _, metric_damp, metric_lap, _, _ = study(1 + n)
                value = shift_grad[i][j] + shift_grad[j][i] - 2.0 * free
                if i == j:
                    value = value - (2.0 / 3.0) * spread
                finish(1 + n, value + metric_damp)
                ricci.append(
                    0.5 * (gamma_grad[i][j] + gamma_grad[j][i] - metric_lap) - hessian[(i, j)]
                )
            trace = (ricci[0] + ricci[3] + ricci[5]) * (1.0 / 3.0)
            for n, (i, j) in enumerate(PAIRS):
                value = ricci[n] - trace if i == j else ricci[n]
                finish(8 + n, value + free_damp[n])
            return c

        lax.fori_loop(0, 8, slab, 0)
        for number, route in enumerate(ROUTES):

            @pl.when(present(route))
            def _(number=number):
                message(number, slot).wait_send()

        return carry

    lax.fori_loop(0, 4, stage, 0)

    def hand_out(f, carry):
        for x in range(8):
            out_ref[f, x] = acc[f, x]
        return carry

    lax.fori_loop(0, fields, hand_out, 0)


def advance(start):
    fields, width, height, depth = start.shape
    groups = fields * width // 32
    tall = height + 16

    def buffer(*sizes):
        return pltpu.VMEM(sizes + (depth,), jnp.float32)

    return pl.pallas_call(
        step_kernel,
        out_shape=jax.ShapeDtypeStruct(start.shape, jnp.float32),
        in_specs=[pl.BlockSpec(memory_space=pltpu.VMEM)],
        out_specs=pl.BlockSpec(memory_space=pltpu.VMEM),
        scratch_shapes=[
            buffer(2, fields, width + 6, tall),
            buffer(fields, width + 4, tall),
            buffer(fields, width, height),
            buffer(3, tall),
            buffer(2, 2, 3, fields, width),
            buffer(2, 2, 3, fields, width),
            buffer(2, 2, MIXED, width),
            buffer(2, 2, 2, MIXED, width),
            buffer(2, 2, groups, height),
            buffer(2, 2, groups, height),
            buffer(2, 2, 2, 2, height),
            buffer(2, 2, 2, 2, height),
            pltpu.SemaphoreType.DMA((len(ROUTES),)),
            pltpu.SemaphoreType.DMA((2, len(ROUTES))),
        ],
        compiler_params=pltpu.CompilerParams(
            collective_id=0, has_side_effects=True, vmem_limit_bytes=48 * 1024 * 1024
        ),
    )(start)


def lagrange(shift, rows, cols):
    spots = jnp.arange(rows, dtype=jnp.int32) + shift
    first_col = spots // 2 + spots % 2
    odd_spot = spots % 2 == 1
    columns = jnp.arange(cols, dtype=jnp.int32)
    matrix = jnp.zeros((rows, cols), jnp.float32)
    for t in range(4):
        weight = jnp.where(odd_spot, ODD_W[t], EVEN_W[t])
        matrix = matrix + jnp.where(
            columns[None, :] == (first_col + t)[:, None], weight[:, None], 0.0
        )
    return matrix


def body(state, coarse_bricks, shifts, brick_owner):
    fields, width, height, depth = state.shape
    brick_side = width + 4
    brick_depth = depth // 2 + 4
    shift_x = shifts[0]
    shift_y = shifts[1]
    beyond_x = passed_along(state, "gx", -1)
    moved = lax.dynamic_slice_in_dim(
        jnp.concatenate([state, beyond_x], axis=1), shift_x, width, axis=1
    )
    beyond_y = passed_along(moved, "gy", -1)
    moved = lax.dynamic_slice_in_dim(
        jnp.concatenate([moved, beyond_y], axis=2), shift_y, height, axis=2
    )
    place_x = lax.axis_index("gx")
    place_y = lax.axis_index("gy")
    wanted = jnp.sum(
        jnp.where(jnp.arange(brick_owner.shape[0], dtype=jnp.int32) == place_x, brick_owner, 0)
    )
    piece = lax.all_gather(coarse_bricks, "gx", axis=0, tiled=True)
    chosen = (jnp.arange(piece.shape[0], dtype=jnp.int32) == wanted).astype(jnp.float32)
    flat_brick = jnp.sum(piece[:, 0, 0] * chosen[:, None], axis=0)
    brick = flat_brick.reshape((fields, brick_side, brick_side, brick_depth))
    along_x = lagrange(shift_x, width, brick_side)
    along_y = lagrange(shift_y, height, brick_side)
    along_z = lagrange(jnp.zeros((), jnp.int32), depth, brick_depth)
    first_pass = jnp.einsum("fpqr,kr->fpqk", brick, along_z, precision=HIGH)
    second_pass = jnp.einsum("fpqk,jq->fpjk", first_pass, along_y, precision=HIGH)
    refill = jnp.einsum("fpjk,ip->fijk", second_pass, along_x, precision=HIGH)
    rows = place_x * width + jnp.arange(width, dtype=jnp.int32)
    cols = place_y * height + jnp.arange(height, dtype=jnp.int32)
    entering = (rows + shift_x >= width * lax.axis_size("gx"))[:, None] | (
        cols + shift_y >= height * lax.axis_size("gy")
    )[None, :]
    start = jnp.where(entering[None, :, :, None], refill, moved)
    return advance(start)


def solution(mesh):
    return jax.shard_map(
        body,
        mesh=mesh,
        in_specs=(P(None, "gx", "gy", "gz"), P("gx", "gy", "gz", None), P(), P()),
        out_specs=P(None, "gx", "gy", "gz"),
        check_vma=False,
    )
```

profile of v0, /device:TPU:0, one launch (start us, length us, event | category | flops | bytes accessed | tf_op | source)
XLA Modules:
  0.0 152.6 jit_solution(14068919023159920545)
XLA Ops:
  6.5 0.0 all-gather.2.cloned.1.call-start
  6.5 0.7 all-gather.2.cloned.1.call-update
  7.3 1.3 collective-permute-start
  8.6 1.3 fusion.65
  9.9 0.6 broadcast_select_fusion.4
  10.5 0.6 broadcast_select_fusion.8
  11.1 0.6 broadcast_add_fusion.5
  11.6 0.6 fusion.60
  12.2 1.3 fusion.59
  13.6 0.6 compare_convert_fusion
  17.8 0.7 fusion.61
  18.5 0.7 broadcast_select_fusion.6
  19.2 0.7 broadcast_select_fusion.10
  19.8 0.7 broadcast_add_fusion.6
  20.5 1.2 add_compare_fusion
  21.7 0.1 broadcast_or_fusion
  21.8 0.0 collective-permute-done
  21.8 1.0 fusion.5
  22.8 1.3 collective-permute-start.1
  24.1 19.9 %all-gather.2.cloned.1.call-done = f32[4,1,1,235008]{3,2,1,0:T(1,128)} async-done(((f32[1,1,1,235008]{3,2,1,0:T(1,128)}), f32[4,1,1,235008]{3,2,1,0:T(1,128)}) %all-gather.2.cloned.1.call-update) | async-done | bytes 3760144 | tf_op jit(solution)/shard_map/all_gather | solution.py:477
  44.0 11.3 %fusion = f32[235008]{0:T(1024)S(1)} fusion(f32[4,1,1,235008]{3,2,1,0:T(1,128)} %all-gather.2.cloned.1.call-done, f32[4]{0:T(128)S(1)} %compare_convert_fusion), kind=kLoop, calls=%fused_computation.1 | loop fusion | flops 1645056 | bytes 4700176 | tf_op jit(solution)/shard_map/reduce_sum | solution.py:479
  55.4 1.5 reshape.200
  56.9 2.1 %fusion.6 = f32[24,12,12,128]{3,2,1,0:T(8,128)S(1)} fusion(f32[24,12,12,68]{3,2,1,0:T(8,128)S(1)} %reshape.200, f32[128]{0:T(128)S(1)} %get-tuple-element.21, s32[128]{0:T(128)S(1)} %get-tuple-element.16, f32[128]{0:T(128)S(1)} %get-tuple-element.19, s32[128]{0:T(128)S(1)} %get-tuple-element.23, f32[128]{0:T(128)S(1)} %get-tuple-element.20, ...), kind=kOutput, calls=%fused_computation.16 | convolution fusion | flops 361068032 | bytes 2713600 | tf_op jit(solution)/shard_map/fpqr,kr->fpqk/dot_general | solution.py:484
  59.0 1.3 convolution_bitcast_fusion
  60.3 1.0 fusion.1
  61.3 0.0 collective-permute-done.1
  61.3 1.8 %fusion.4.start_ref = f32[24,8,8,128]{3,2,1,0:T(8,128)S(1)} fusion(s32[]{:T(128)S(6)} %select_n.320, f32[24,8,8,128]{3,2,1,0:T(8,128)} %fusion.5, f32[24,8,8,128]{3,2,1,0:T(8,128)} %collective-permute-done.1, f32[8,24,8,128]{3,0,2,1:T(8,128)S(1)} %fusion.1, pred[8,8]{1,0:T(8,128)(4,1)S(1)} %broadcast_or_fusion), kind=kLoop, calls=%fused_computation.10 | loop fusion | flops 393216 | bytes 3145796 | tf_op jit(solution)/shard_map/jit(_where)/select_n | solution.py:492
  63.1 81.8 %shard_map.46 = f32[24,8,8,128]{3,2,1,0:T(8,128)S(1)} custom-call(f32[24,8,8,128]{3,2,1,0:T(8,128)S(1)} %fusion.4.start_ref), custom_call_target="tpu_custom_call" | custom-call | tf_op jit(solution)/shard_map/pallas_call | solution.py:417
  144.9 0.9 copy.18
  (4 shorter events, 0.0 us)
Async XLA Ops:
  6.5 37.5 %all-gather.2.cloned.1.call-start = ((), (), s32[]{:S(2)}) async-start(), calls=%async_computation | async-start | bytes 4700160 | tf_op jit(solution)/shard_map/all_gather | solution.py:477
  7.3 14.5 %collective-permute-start = (f32[24,8,8,128]{3,2,1,0:T(8,128)}, f32[24,8,8,128]{3,2,1,0:T(8,128)S(1)}, u32[]{:S(2)}, u32[]{:S(2)}) collective-permute-start(f32[24,8,8,128]{3,2,1,0:T(8,128)} %param.4), channel_id=1, source_target_pairs={{8,0},{16,8},{24,16},{9,1},{17,9},{25,17},{10,2},{18,10},{26,18},{... | collective-permute-start | bytes 2359304 | tf_op jit(solution)/shard_map/ppermute | solution.py:20
  22.8 38.5 %collective-permute-start.1 = (f32[24,8,8,128]{3,2,1,0:T(8,128)}, f32[24,8,8,128]{3,2,1,0:T(8,128)}, u32[]{:S(2)}, u32[]{:S(2)}) collective-permute-start(f32[24,8,8,128]{3,2,1,0:T(8,128)} %fusion.5), channel_id=1, source_target_pairs={{4,0},{5,1},{6,2},{7,3},{12,8},{13,9},{14,10},{15,11},{20,16},{21,... | collective-permute-start | bytes 2359304 | tf_op jit(solution)/shard_map/ppermute | solution.py:20
Sparse Core Ops, SparseCore 0:
  8.9 35.0 all-gather.1
where the time goes:
time: 153 us
  Pallas kernels  81.8 us (53%)
  other arithmetic  22.4 us (15%)
  waiting for transfers between devices  20.6 us (13%)
  between operations  17.2 us (11%)
  matrix products  4.4 us (3%)
  local copies, waits for them, and re-layouts  3.71 us (2%)
  starting transfers between devices  2.57 us (2%)
    pallas_call x1, Pallas kernels, advance(): pl.pallas_call(step_kernel, out_shape=jax.ShapeDtypeStruct(start.shape, j...  81.8 us
    all_gather x1, waiting for transfers between devices, body(): piece = lax.all_gather(coarse_bricks, 'gx', axis=0, tiled=True)  19.9 us
    reduce_sum x1, other arithmetic, body(): flat_brick = jnp.sum(piece[:, 0, 0] * chosen[:, None], axis=0)  11.3 us
  transfers between devices with their start and end apart: 3, of which 1 were waited for; matrix products, arithmetic and copies ran while one was open for 18% of the time, Pallas kernels for 0%

commit v1 on v0

--- a/solution.py
+++ b/solution.py
@@ -1,5 +1,6 @@
 import jax
 import jax.numpy as jnp
+import numpy as np
 from jax import lax
 from jax.experimental import pallas as pl
 from jax.experimental.pallas import tpu as pltpu
@@ -24,6 +25,7 @@
 ORDER = (0, 17, 18, 19, 20, 1, 2, 3, 4, 5, 6, 7, 8, 9, 10, 11, 12, 13, 14, 15, 16, 21, 22, 23)
 PLACE = {field: place for place, field in enumerate(ORDER)}
 MIXED = 5
+PORTIONS = 6
 FACES = tuple(
     tuple(side if d == axis else 0 for d in range(3)) for axis in range(3) for side in (-1, 1)
 )
@@ -42,10 +44,11 @@
 
 
 def step_kernel(
-    start_ref, out_ref, box, zhalo, acc, slopes, ysend, yrecv, csend, crecv, zsend, zcore, zx, zy,
-    send_sem, recv_sem,
+    shifts_ref, source_ref, moved_ref, filled_ref, out_ref, start_ref, gathered, box, zhalo, acc, slopes, ysend, yrecv, csend, crecv, zsend, zcore, zx, zy,
+    send_sem, recv_sem, own_send, own_recv, far_send, far_recv, on_send, on_recv,
 ):
     fields = start_ref.shape[0]
+    portion = fields // PORTIONS
     groups = zsend.shape[2]
     counts = tuple(lax.axis_size(name) for name in ("gx", "gy", "gz"))
     place = tuple(lax.axis_index(name) for name in ("gx", "gy", "gz"))
@@ -72,15 +75,15 @@
             for x in range(14):
                 for y in (0, 16) if 3 <= x < 11 else (0, 8, 16):
                     box[slot, f, x, pl.ds(y, 8), :] = zero
+        return carry
+
+    lax.fori_loop(0, fields, wipe_field, 0)
+
+    def keep_own(f, carry):
         for x in range(8):
-            value = start_ref[f, x]
-            acc[f, x] = value
+            gathered[0, f, x] = filled_ref[f, x]
         return carry
 
-    lax.fori_loop(0, fields, wipe_field, 0)
-    for f in range(fields):
-        for x in range(8):
-            box[0, f, 3 + x, pl.ds(8, 8), :] = start_ref[ORDER[f], x]
     for slot in range(2):
         for z in range(2):
             for g in range(groups):
@@ -103,7 +106,11 @@
     lax.fori_loop(0, fields, wipe_y, 0)
 
     barrier = pltpu.get_barrier_semaphore()
-    total = jnp.int32(0)
+    partner = (place[0] + 1 - 2 * lax.rem(place[0], 2), place[1], place[2])
+    across = (lax.rem(place[0] + 2, 4), place[1], place[2])
+    total = jnp.int32(2)
+    for other in (partner, across):
+        pl.semaphore_signal(barrier, inc=1, device_id=other, device_id_type=MESH)
     for route in ROUTES:
         ok = present(route)
         total = total + ok.astype(jnp.int32)
@@ -113,6 +120,53 @@
             pl.semaphore_signal(barrier, inc=1, device_id=peer(route), device_id_type=MESH)
 
     pl.semaphore_wait(barrier, total)
+
+    def remote(source, target, sent, got, device):
+        return pltpu.make_async_remote_copy(
+            src_ref=source,
+            dst_ref=target,
+            send_sem=sent,
+            recv_sem=got,
+            device_id=device,
+            device_id_type=MESH,
+        )
+
+    def far_copy(k):
+        part = pl.ds(k * portion, portion)
+        return remote(
+            filled_ref.at[part], gathered.at[2, part], far_send.at[k], far_recv.at[k], across
+        )
+
+    def on_copy(k):
+        part = pl.ds(k * portion, portion)
+        return remote(
+            gathered.at[2, part], gathered.at[3, part], on_send.at[k], on_recv.at[k], partner
+        )
+
+    own_copy = remote(filled_ref, gathered.at[1], own_send, own_recv, partner)
+    for k in range(PORTIONS):
+        far_copy(k).start()
+    own_copy.start()
+    lax.fori_loop(0, fields, keep_own, 0)
+    for k in range(PORTIONS):
+        far_copy(k).wait_recv()
+        on_copy(k).start()
+    own_copy.wait()
+    for k in range(PORTIONS):
+        on_copy(k).wait()
+        far_copy(k).wait_send()
+    chosen = source_ref[0]
+    row_spot = row + (place[1] * 8 + shifts_ref[1])
+    column_entering = row_spot >= 8 * counts[1]
+    for f in range(fields):
+        for x in range(8):
+            x_spot = jnp.zeros((8, 128), jnp.int32) + (place[0] * 8 + x + shifts_ref[0])
+            entering = jnp.logical_or(column_entering, x_spot >= 8 * counts[0])
+            name = ORDER[f]
+            value = jnp.where(entering, gathered[chosen, name, x], moved_ref[name, x])
+            start_ref[name, x] = value
+            acc[name, x] = value
+            box[0, f, 3 + x, pl.ds(8, 8), :] = value
 
     def message(number, slot):
         route = ROUTES[number]
@@ -406,8 +460,8 @@
     lax.fori_loop(0, fields, hand_out, 0)
 
 
-def advance(start):
-    fields, width, height, depth = start.shape
+def advance(shifts, source, moved, filled):
+    fields, width, height, depth = moved.shape
     groups = fields * width // 32
     tall = height + 16
 
@@ -416,10 +470,13 @@
 
     return pl.pallas_call(
         step_kernel,
-        out_shape=jax.ShapeDtypeStruct(start.shape, jnp.float32),
-        in_specs=[pl.BlockSpec(memory_space=pltpu.VMEM)],
+        out_shape=jax.ShapeDtypeStruct(moved.shape, jnp.float32),
+        in_specs=[pl.BlockSpec(memory_space=pltpu.SMEM)] * 2
+        + [pl.BlockSpec(memory_space=pltpu.VMEM)] * 2,
         out_specs=pl.BlockSpec(memory_space=pltpu.VMEM),
         scratch_shapes=[
+            buffer(fields, width, height),
+            buffer(4, fields, width, height),
             buffer(2, fields, width + 6, tall),
             buffer(fields, width + 4, tall),
             buffer(fields, width, height),
@@ -434,25 +491,33 @@
             buffer(2, 2, 2, 2, height),
             pltpu.SemaphoreType.DMA((len(ROUTES),)),
             pltpu.SemaphoreType.DMA((2, len(ROUTES))),
+            pltpu.SemaphoreType.DMA,
+            pltpu.SemaphoreType.DMA,
+            pltpu.SemaphoreType.DMA((PORTIONS,)),
+            pltpu.SemaphoreType.DMA((PORTIONS,)),
+            pltpu.SemaphoreType.DMA((PORTIONS,)),
+            pltpu.SemaphoreType.DMA((PORTIONS,)),
         ],
         compiler_params=pltpu.CompilerParams(
             collective_id=0, has_side_effects=True, vmem_limit_bytes=48 * 1024 * 1024
         ),
-    )(start)
+    )(shifts, source, moved, filled)
 
 
 def lagrange(shift, rows, cols):
-    spots = jnp.arange(rows, dtype=jnp.int32) + shift
-    first_col = spots // 2 + spots % 2
-    odd_spot = spots % 2 == 1
-    columns = jnp.arange(cols, dtype=jnp.int32)
-    matrix = jnp.zeros((rows, cols), jnp.float32)
-    for t in range(4):
-        weight = jnp.where(odd_spot, ODD_W[t], EVEN_W[t])
-        matrix = matrix + jnp.where(
-            columns[None, :] == (first_col + t)[:, None], weight[:, None], 0.0
-        )
+    matrix = np.zeros((rows, cols), np.float32)
+    for line in range(rows):
+        spot = line + shift
+        first = spot // 2 + spot % 2
+        for t, weight in enumerate(ODD_W if spot % 2 else EVEN_W):
+            if first + t < cols:
+                matrix[line, first + t] = weight
     return matrix
+
+
+def lagrange_at(shift, rows, cols):
+    table = np.stack([lagrange(s, rows, cols) for s in range(rows + 1)])
+    return lax.dynamic_index_in_dim(jnp.asarray(table), shift, 0, keepdims=False)
 
 
 def body(state, coarse_bricks, shifts, brick_owner):
@@ -470,27 +535,18 @@
         jnp.concatenate([moved, beyond_y], axis=2), shift_y, height, axis=2
     )
     place_x = lax.axis_index("gx")
-    place_y = lax.axis_index("gy")
     wanted = jnp.sum(
         jnp.where(jnp.arange(brick_owner.shape[0], dtype=jnp.int32) == place_x, brick_owner, 0)
     )
-    piece = lax.all_gather(coarse_bricks, "gx", axis=0, tiled=True)
-    chosen = (jnp.arange(piece.shape[0], dtype=jnp.int32) == wanted).astype(jnp.float32)
-    flat_brick = jnp.sum(piece[:, 0, 0] * chosen[:, None], axis=0)
-    brick = flat_brick.reshape((fields, brick_side, brick_side, brick_depth))
-    along_x = lagrange(shift_x, width, brick_side)
-    along_y = lagrange(shift_y, height, brick_side)
-    along_z = lagrange(jnp.zeros((), jnp.int32), depth, brick_depth)
+    brick = coarse_bricks.reshape((fields, brick_side, brick_side, brick_depth))
+    along_x = lagrange_at(shift_x, width, brick_side)
+    along_y = lagrange_at(shift_y, height, brick_side)
+    along_z = jnp.asarray(lagrange(0, depth, brick_depth))
     first_pass = jnp.einsum("fpqr,kr->fpqk", brick, along_z, precision=HIGH)
     second_pass = jnp.einsum("fpqk,jq->fpjk", first_pass, along_y, precision=HIGH)
-    refill = jnp.einsum("fpjk,ip->fijk", second_pass, along_x, precision=HIGH)
-    rows = place_x * width + jnp.arange(width, dtype=jnp.int32)
-    cols = place_y * height + jnp.arange(height, dtype=jnp.int32)
-    entering = (rows + shift_x >= width * lax.axis_size("gx"))[:, None] | (
-        cols + shift_y >= height * lax.axis_size("gy")
-    )[None, :]
-    start = jnp.where(entering[None, :, :, None], refill, moved)
-    return advance(start)
+    filled = jnp.einsum("fpjk,ip->fijk", second_pass, along_x, precision=HIGH)
+    source = jnp.bitwise_xor(wanted, place_x).astype(jnp.int32).reshape(1)
+    return advance(shifts, source, moved, filled)
 
 
 def solution(mesh):

time: 153 us -> 150 us (0.980)
  Pallas kernels: 81.8 us -> 104 us
  other arithmetic: 22.4 us -> 11.6 us
  between operations: 17.2 us -> 6.68 us
  waiting for transfers between devices: 20.6 us -> 14.5 us
  matrix products: 4.4 us -> 6.29 us
    pallas_call x1, Pallas kernels: 81.8 us -> 104 us  [advance(): pl.pallas_call(step_kernel, out_shape=jax.ShapeDtypeStruct(moved.shape, j...]
    all_gather x1 -> x0, waiting for transfers between devices: 19.9 us -> none  [body(): piece = lax.all_gather(coarse_bricks, 'gx', axis=0, tiled=True)]
    ppermute x2, waiting for transfers between devices: 0.01 us -> 14.5 us  [passed_along(): return lax.ppermute(block, axis, route)]
    reduce_sum x1 -> x0, other arithmetic: 11.3 us -> none  [body(): flat_brick = jnp.sum(piece[:, 0, 0] * chosen[:, None], axis=0)]
    unnamed x0 -> x1, other arithmetic: none -> 8.8 us
    select_n x7 -> x0, other arithmetic: 4.26 us -> none  [the longest x6 2.47 us: lagrange(): weight = jnp.where(odd_spot, ODD_W[t], EVEN_W[t])]
    add x6 -> x0, other arithmetic: 2.49 us -> none  [the longest x3 1.25 us: lagrange(): first_col + t]
  transfers between devices with their start and end apart: 3 -> 2, of which waited for: 1 -> 1; matrix products, arithmetic and copies ran while one was open for 18% -> 13% of each run, Pallas kernels for 0% -> 0%
where the time goes in v1:
time: 150 us
  Pallas kernels  104 us (69%)
  waiting for transfers between devices  14.5 us (10%)
  other arithmetic  11.6 us (8%)
  between operations  6.68 us (4%)
  matrix products  6.29 us (4%)
  local copies, waits for them, and re-layouts  3.86 us (3%)
  starting transfers between devices  2.57 us (2%)
    pallas_call x1, Pallas kernels, advance(): pl.pallas_call(step_kernel, out_shape=jax.ShapeDtypeStruct(moved.shape, j...  104 us
    ppermute x2, waiting for transfers between devices, passed_along(): return lax.ppermute(block, axis, route)  14.5 us
    unnamed x1, other arithmetic  8.8 us
  transfers between devices with their start and end apart: 2, of which 1 were waited for; matrix products, arithmetic and copies ran while one was open for 13% of the time, Pallas kernels for 0%

profile of v1, /device:TPU:0, one launch (start us, length us, event | category | flops | bytes accessed | tf_op | source)
XLA Modules:
  0.0 149.7 jit_solution(5660153461445740263)
XLA Ops:
  0.0 1.3 collective-permute-start
  1.3 1.3 fusion.21
  6.1 1.3 fusion.20
  10.5 8.8 %reduce = f32[235008]{0:T(1024)S(1)} reduce(f32[1,1,1,235008]{3,2,1,0:T(1,128)} %param.8, f32[]{:T(128)} %constant.24), dimensions={0,1,2}, to_apply=%param.8.reduce_sub_computation | reduce | bytes 1880068 | tf_op args[1]
  19.3 1.5 %reshape.7 = f32[24,12,12,68]{3,2,1,0:T(8,128)S(1)} reshape(f32[235008]{0:T(1024)S(1)} %reduce) | data formatting | bytes 1880064 | tf_op jit(solution)/shard_map/reshape | solution.py:541
  20.8 0.0 copy-start.1
  20.8 0.0 collective-permute-done
  20.8 1.3 fusion.13
  22.1 1.3 collective-permute-start.1
  23.4 0.0 copy-done.1
  23.4 2.5 %fusion.6 = f32[24,12,12,128]{3,0,2,1:T(8,128)S(1)} fusion(f32[128,68,1,1]{0,1,3,2:T(8,128)S(1)} %copy-done.1, f32[24,12,12,68]{3,2,1,0:T(8,128)S(1)} %reshape.7), kind=kOutput, calls=%fused_computation.10 | convolution fusion | flops 360972288 | bytes 2744320 | tf_op jit(solution)/shard_map/fpqr,kr->fpqk/dot_general | solution.py:545
  25.9 2.1 %fusion.9 = f32[24,12,8,128]{3,2,1,0:T(8,128)S(1)} fusion(f32[24,12,12,128]{3,0,2,1:T(8,128)S(1)} %fusion.6, f32[9,8,12]{2,1,0:T(8,128)} %constant.20.clone, s32[]{:T(128)S(6)} %select_n.21), kind=kOutput, calls=%fused_computation.11 | convolution fusion | flops 42467328 | bytes 2953220 | tf_op jit(solution)/shard_map/fpqk,jq->fpjk/dot_general | solution.py:546
  28.0 1.7 %fusion.4 = f32[8,24,8,128]{3,0,2,1:T(8,128)S(1)} fusion(f32[24,12,8,128]{3,2,1,0:T(8,128)S(1)} %fusion.9, f32[9,8,12]{2,1,0:T(8,128)} %constant.20.clone, s32[]{:T(128)S(6)} %select_n.20), kind=kOutput, calls=%fused_computation.8 | convolution fusion | flops 28311552 | bytes 1970180 | tf_op jit(solution)/shard_map/fpjk,ip->fijk/dot_general | solution.py:547
  29.7 0.0 copy-start
  29.7 0.1 copy.28
  29.9 14.5 %collective-permute-done.1 = f32[24,8,8,128]{3,2,1,0:T(8,128)S(1)} collective-permute-done((f32[24,8,8,128]{3,2,1,0:T(8,128)S(1)}, f32[24,8,8,128]{3,2,1,0:T(8,128)S(1)}, u32[]{:S(2)}, u32[]{:S(2)}) %collective-permute-start.1) | collective-permute-done | bytes 786464 | tf_op jit(solution)/shard_map/ppermute | solution.py:21
  44.4 0.2 fusion.12.moved_ref
  44.6 0.0 copy-done
  44.6 104.3 %shard_map.73 = f32[24,8,8,128]{3,2,1,0:T(8,128)S(1)} custom-call(s32[2]{0:T(128)S(1)} %copy-done, s32[1]{0:T(128)} %bitcast.source_ref, f32[24,8,8,128]{3,2,1,0:T(8,128)S(1)} %fusion.12.moved_ref, f32[24,8,8,128]{3,2,1,0:T(8,128)S(1)} %bitcast.28), custom_call_target="tpu_custom_call" | custom-call | tf_op jit(solution)/shard_map/pallas_call | solution.py:471
  148.9 0.9 copy.30
Async XLA Ops:
  0.0 20.8 %collective-permute-start = (f32[24,8,8,128]{3,2,1,0:T(8,128)}, f32[24,8,8,128]{3,2,1,0:T(8,128)}, u32[]{:S(2)}, u32[]{:S(2)}) collective-permute-start(f32[24,8,8,128]{3,2,1,0:T(8,128)} %param.7), channel_id=1, source_target_pairs={{8,0},{16,8},{24,16},{9,1},{17,9},{25,17},{10,2},{18,10},{26,18},{... | collective-permute-start | bytes 2359304 | tf_op jit(solution)/shard_map/ppermute | solution.py:21
  20.8 2.6 %copy-start.1 = (f32[128,68,1,1]{0,1,3,2:T(8,128)S(1)}, f32[128,68,1,1]{0,1,3,2:T(8,128)}, u32[]{:S(2)}) copy-start(f32[128,68,1,1]{0,1,3,2:T(8,128)} %constant.23) | copy-start | bytes 104452
  22.1 22.3 %collective-permute-start.1 = (f32[24,8,8,128]{3,2,1,0:T(8,128)S(1)}, f32[24,8,8,128]{3,2,1,0:T(8,128)S(1)}, u32[]{:S(2)}, u32[]{:S(2)}) collective-permute-start(f32[24,8,8,128]{3,2,1,0:T(8,128)S(1)} %fusion.13), channel_id=1, source_target_pairs={{4,0},{5,1},{6,2},{7,3},{12,8},{13,9},{14,10},{15,11},{20,16},{21,... | collective-permute-start | bytes 2359304 | tf_op jit(solution)/shard_map/ppermute | solution.py:21
  29.7 14.9 %copy-start = (s32[2]{0:T(128)S(1)}, s32[2]{0:T(128)}, u32[]{:S(2)}) copy-start(s32[2]{0:T(128)} %shifts_ref.1) | copy-start | bytes 28

commit v2 on v1

--- a/solution.py
+++ b/solution.py
@@ -44,8 +44,8 @@
 
 
 def step_kernel(
-    shifts_ref, source_ref, moved_ref, filled_ref, out_ref, start_ref, gathered, box, zhalo, acc, slopes, ysend, yrecv, csend, crecv, zsend, zcore, zx, zy,
-    send_sem, recv_sem, own_send, own_recv, far_send, far_recv, on_send, on_recv,
+    shifts_ref, source_ref, moved_ref, filled_ref, out_ref, start_ref, gathered, column, box, zhalo, acc, slopes, ysend, yrecv, csend, crecv, zsend, zcore, zx, zy,
+    send_sem, recv_sem, own_send, own_recv, far_send, far_recv, on_send, on_recv, y_send, y_recv,
 ):
     fields = start_ref.shape[0]
     portion = fields // PORTIONS
@@ -79,9 +79,19 @@
 
     lax.fori_loop(0, fields, wipe_field, 0)
 
+    @pl.when(place[1] == counts[1] - 1)
+    def _():
+        def wipe_column(f, carry):
+            for x in range(8):
+                column[f, x, pl.ds(8, 8), :] = zero
+            return carry
+
+        lax.fori_loop(0, fields, wipe_column, 0)
+
     def keep_own(f, carry):
         for x in range(8):
             gathered[0, f, x] = filled_ref[f, x]
+            column[f, x, pl.ds(0, 8), :] = moved_ref[f, x]
         return carry
 
     for slot in range(2):
@@ -144,6 +154,18 @@
         )
 
     own_copy = remote(filled_ref, gathered.at[1], own_send, own_recv, partner)
+    y_copy = remote(
+        moved_ref,
+        column.at[:, :, pl.ds(8, 8), :],
+        y_send,
+        y_recv,
+        (place[0], place[1] - 1, place[2]),
+    )
+
+    @pl.when(place[1] > 0)
+    def _():
+        y_copy.start()
+
     for k in range(PORTIONS):
         far_copy(k).start()
     own_copy.start()
@@ -155,7 +177,17 @@
     for k in range(PORTIONS):
         on_copy(k).wait()
         far_copy(k).wait_send()
+
+    @pl.when(place[1] > 0)
+    def _():
+        y_copy.wait_send()
+
+    @pl.when(place[1] < counts[1] - 1)
+    def _():
+        y_copy.wait_recv()
+
     chosen = source_ref[0]
+    shift_y = shifts_ref[1]
     row_spot = row + (place[1] * 8 + shifts_ref[1])
     column_entering = row_spot >= 8 * counts[1]
     for f in range(fields):
@@ -163,7 +195,7 @@
             x_spot = jnp.zeros((8, 128), jnp.int32) + (place[0] * 8 + x + shifts_ref[0])
             entering = jnp.logical_or(column_entering, x_spot >= 8 * counts[0])
             name = ORDER[f]
-            value = jnp.where(entering, gathered[chosen, name, x], moved_ref[name, x])
+            value = jnp.where(entering, gathered[chosen, name, x], column[name, x, pl.ds(shift_y, 8), :])
             start_ref[name, x] = value
             acc[name, x] = value
             box[0, f, 3 + x, pl.ds(8, 8), :] = value
@@ -477,6 +509,7 @@
         scratch_shapes=[
             buffer(fields, width, height),
             buffer(4, fields, width, height),
+            buffer(fields, width, 2 * height),
             buffer(2, fields, width + 6, tall),
             buffer(fields, width + 4, tall),
             buffer(fields, width, height),
@@ -497,6 +530,8 @@
             pltpu.SemaphoreType.DMA((PORTIONS,)),
             pltpu.SemaphoreType.DMA((PORTIONS,)),
             pltpu.SemaphoreType.DMA((PORTIONS,)),
+            pltpu.SemaphoreType.DMA,
+            pltpu.SemaphoreType.DMA,
         ],
         compiler_params=pltpu.CompilerParams(
             collective_id=0, has_side_effects=True, vmem_limit_bytes=48 * 1024 * 1024
@@ -518,6 +553,22 @@
 def lagrange_at(shift, rows, cols):
     table = np.stack([lagrange(s, rows, cols) for s in range(rows + 1)])
     return lax.dynamic_index_in_dim(jnp.asarray(table), shift, 0, keepdims=False)
+
+
+def flatten_kernel(bricks_ref, flat_ref, sem):
+    copy = pltpu.make_async_copy(bricks_ref.at[0, 0, 0], flat_ref, sem)
+    copy.start()
+    copy.wait()
+
+
+def flattened(bricks):
+    return pl.pallas_call(
+        flatten_kernel,
+        out_shape=jax.ShapeDtypeStruct((bricks.size,), jnp.float32),
+        in_specs=[pl.BlockSpec(memory_space=pl.ANY)],
+        out_specs=pl.BlockSpec(memory_space=pl.ANY),
+        scratch_shapes=[pltpu.SemaphoreType.DMA],
+    )(bricks)
 
 
 def body(state, coarse_bricks, shifts, brick_owner):
@@ -530,15 +581,11 @@
     moved = lax.dynamic_slice_in_dim(
         jnp.concatenate([state, beyond_x], axis=1), shift_x, width, axis=1
     )
-    beyond_y = passed_along(moved, "gy", -1)
-    moved = lax.dynamic_slice_in_dim(
-        jnp.concatenate([moved, beyond_y], axis=2), shift_y, height, axis=2
-    )
     place_x = lax.axis_index("gx")
     wanted = jnp.sum(
         jnp.where(jnp.arange(brick_owner.shape[0], dtype=jnp.int32) == place_x, brick_owner, 0)
     )
-    brick = coarse_bricks.reshape((fields, brick_side, brick_side, brick_depth))
+    brick = flattened(coarse_bricks).reshape((fields, brick_side, brick_side, brick_depth))
     along_x = lagrange_at(shift_x, width, brick_side)
     along_y = lagrange_at(shift_y, height, brick_side)
     along_z = jnp.asarray(lagrange(0, depth, brick_depth))

time: 150 us -> 157 us (1.047)
  Pallas kernels: 104 us -> 135 us
  waiting for transfers between devices: 14.5 us -> 0.01 us
  other arithmetic: 11.6 us -> 0.81 us
  matrix products: 6.29 us -> 8 us
    pallas_call x0 -> x1, Pallas kernels: none -> 29.6 us  [flattened(): pl.pallas_call(flatten_kernel, out_shape=jax.ShapeDtypeStruct((bricks.siz...]
    ppermute x2 -> x1, waiting for transfers between devices: 14.5 us -> 0.01 us  [passed_along(): return lax.ppermute(block, axis, route)]
    unnamed x1 -> x0, other arithmetic: 8.8 us -> none
    reshape x1, local copies, waits for them, and re-layouts: 1.51 us -> 3.48 us  [body(): flattened(coarse_bricks)]
    dot_general x1, matrix products: 2.47 us -> 4.1 us  [body(): first_pass = jnp.einsum('fpqr,kr->fpqk', brick, along_z, precision=HIGH)]
  transfers between devices with their start and end apart: 2 -> 1, of which waited for: 1 -> 0; matrix products, arithmetic and copies ran while one was open for 13% -> 8% of each run, Pallas kernels for 0% -> 19%
where the time goes in v2:
time: 157 us; the launch traced here: 156 us
  Pallas kernels  135 us (86%)
  matrix products  8 us (5%)
  between operations  5.77 us (4%)
  local copies, waits for them, and re-layouts  5.11 us (3%)
    pallas_call x1, Pallas kernels, advance(): pl.pallas_call(step_kernel, out_shape=jax.ShapeDtypeStruct(moved.shape, j...  106 us
    pallas_call x1, Pallas kernels, flattened(): pl.pallas_call(flatten_kernel, out_shape=jax.ShapeDtypeStruct((bricks.siz...  29.6 us
    dot_general x1, matrix products, body(): first_pass = jnp.einsum('fpqr,kr->fpqk', brick, along_z, precision=HIGH)  4.1 us
    reshape x1, local copies, waits for them, and re-layouts, body(): flattened(coarse_bricks)  3.48 us
  transfers between devices with their start and end apart: 1, of which 0 were waited for; matrix products, arithmetic and copies ran while one was open for 8% of the time, Pallas kernels for 19%

profile of v2, /device:TPU:0, one launch (start us, length us, event | category | flops | bytes accessed | tf_op | source)
XLA Modules:
  0.0 156.3 jit_solution(17313365834755381227)
XLA Ops:
  0.0 1.3 collective-permute-start
  1.3 29.6 %shard_map.73 = f32[235008]{0:T(1024)} custom-call(f32[1,1,1,235008]{3,2,1,0:T(1,128)} %bricks_ref.1), custom_call_target="tpu_custom_call" | custom-call | tf_op jit(solution)/shard_map/pallas_call | solution.py:565
  30.9 0.0 copy-start.2
  30.9 3.5 %reshape.7 = f32[24,12,12,68]{3,2,1,0:T(8,128)} reshape(f32[235008]{0:T(1024)} %shard_map.73) | data formatting | bytes 1880064 | tf_op jit(solution)/shard_map/reshape | solution.py:588
  34.4 0.0 copy-done.2
  34.4 0.0 copy-start
  34.4 4.1 %fusion.6 = f32[24,12,12,128]{3,0,2,1:T(8,128)S(1)} fusion(f32[128,68,1,1]{0,1,3,2:T(8,128)S(1)} %copy-done.2, f32[24,12,12,68]{3,2,1,0:T(8,128)} %reshape.7), kind=kOutput, calls=%fused_computation.8 | convolution fusion | flops 360972288 | bytes 2744320 | tf_op jit(solution)/shard_map/fpqr,kr->fpqk/dot_general | solution.py:592
  38.5 0.0 copy-done
  38.5 0.6 fusion.20
  42.9 2.1 %fusion.9 = f32[24,12,8,128]{3,2,1,0:T(8,128)S(1)} fusion(f32[24,12,12,128]{3,0,2,1:T(8,128)S(1)} %fusion.6, f32[9,8,12]{2,1,0:T(8,128)} %constant.20.clone, s32[]{:T(128)S(6)} %select_n.17), kind=kOutput, calls=%fused_computation.9 | convolution fusion | flops 42467328 | bytes 2953220 | tf_op jit(solution)/shard_map/fpqk,jq->fpjk/dot_general | solution.py:593
  45.0 0.0 copy-start.3
  45.0 0.0 copy-start.1
  45.0 1.8 %fusion.4 = f32[8,24,8,128]{3,0,2,1:T(8,128)S(1)} fusion(f32[24,12,8,128]{3,2,1,0:T(8,128)S(1)} %fusion.9, f32[9,8,12]{2,1,0:T(8,128)} %constant.20.clone, s32[]{:T(128)S(6)} %select_n.16), kind=kOutput, calls=%fused_computation.6 | convolution fusion | flops 28311552 | bytes 1970180 | tf_op jit(solution)/shard_map/fpjk,ip->fijk/dot_general | solution.py:594
  46.8 0.1 copy.28
  48.2 0.0 copy-done.3
  48.2 0.6 fusion.19
  49.5 0.0 collective-permute-done
  49.5 0.0 copy-done.1
  49.5 0.2 fusion.12.moved_ref
  49.7 105.7 %shard_map.74 = f32[24,8,8,128]{3,2,1,0:T(8,128)S(1)} custom-call(s32[2]{0:T(128)S(1)} %copy-done, s32[1]{0:T(128)} %bitcast.source_ref, f32[24,8,8,128]{3,2,1,0:T(8,128)S(1)} %fusion.12.moved_ref, f32[24,8,8,128]{3,2,1,0:T(8,128)S(1)} %bitcast.28), custom_call_target="tpu_custom_call" | custom-call | tf_op jit(solution)/shard_map/pallas_call | solution.py:503
  155.4 0.9 copy.30
Async XLA Ops:
  0.0 49.5 %collective-permute-start = (f32[24,8,8,128]{3,2,1,0:T(8,128)}, f32[24,8,8,128]{3,2,1,0:T(8,128)S(1)}, u32[]{:S(2)}, u32[]{:S(2)}) collective-permute-start(f32[24,8,8,128]{3,2,1,0:T(8,128)} %param.7), channel_id=1, source_target_pairs={{8,0},{16,8},{24,16},{9,1},{17,9},{25,17},{10,2},{18,10},{26,18},{... | collective-permute-start | bytes 2359304 | tf_op jit(solution)/shard_map/ppermute | solution.py:21
  30.9 3.5 %copy-start.2 = (f32[128,68,1,1]{0,1,3,2:T(8,128)S(1)}, f32[128,68,1,1]{0,1,3,2:T(8,128)}, u32[]{:S(2)}) copy-start(f32[128,68,1,1]{0,1,3,2:T(8,128)} %constant.23) | copy-start | bytes 104452
  34.4 4.1 %copy-start = (s32[2]{0:T(128)S(1)}, s32[2]{0:T(128)}, u32[]{:S(2)}) copy-start(s32[2]{0:T(128)} %shifts_ref.1) | copy-start | bytes 28
  45.0 3.2 %copy-start.3 = (s32[4]{0:T(128)S(1)}, s32[4]{0:T(128)}, u32[]{:S(2)}) copy-start(s32[4]{0:T(128)} %param.10) | copy-start | bytes 52
  45.0 4.5 %copy-start.1 = (f32[24,8,8,128]{3,2,1,0:T(8,128)S(1)}, f32[24,8,8,128]{3,2,1,0:T(8,128)}, u32[]{:S(2)}) copy-start(f32[24,8,8,128]{3,2,1,0:T(8,128)} %param.7) | copy-start | bytes 2359300

commit v3 on v2

--- a/solution.py
+++ b/solution.py
@@ -555,22 +555,6 @@
     return lax.dynamic_index_in_dim(jnp.asarray(table), shift, 0, keepdims=False)
 
 
-def flatten_kernel(bricks_ref, flat_ref, sem):
-    copy = pltpu.make_async_copy(bricks_ref.at[0, 0, 0], flat_ref, sem)
-    copy.start()
-    copy.wait()
-
-
-def flattened(bricks):
-    return pl.pallas_call(
-        flatten_kernel,
-        out_shape=jax.ShapeDtypeStruct((bricks.size,), jnp.float32),
-        in_specs=[pl.BlockSpec(memory_space=pl.ANY)],
-        out_specs=pl.BlockSpec(memory_space=pl.ANY),
-        scratch_shapes=[pltpu.SemaphoreType.DMA],
-    )(bricks)
-
-
 def body(state, coarse_bricks, shifts, brick_owner):
     fields, width, height, depth = state.shape
     brick_side = width + 4
@@ -585,7 +569,7 @@
     wanted = jnp.sum(
         jnp.where(jnp.arange(brick_owner.shape[0], dtype=jnp.int32) == place_x, brick_owner, 0)
     )
-    brick = flattened(coarse_bricks).reshape((fields, brick_side, brick_side, brick_depth))
+    brick = coarse_bricks.reshape((fields, brick_side, brick_side, brick_depth))
     along_x = lagrange_at(shift_x, width, brick_side)
     along_y = lagrange_at(shift_y, height, brick_side)
     along_z = jnp.asarray(lagrange(0, depth, brick_depth))

time: 157 us -> 135 us (0.86)
  Pallas kernels: 135 us -> 106 us
  other arithmetic: 0.81 us -> 9.61 us
    pallas_call x1 -> x0, Pallas kernels: 29.6 us -> none  [flattened(): pl.pallas_call(flatten_kernel, out_shape=jax.ShapeDtypeStruct((bricks.siz...]
    unnamed x0 -> x1, other arithmetic: none -> 8.8 us
  transfers between devices with their start and end apart: 1 -> 1, of which waited for: 0 -> 0; matrix products, arithmetic and copies ran while one was open for 8% -> 16% of each run, Pallas kernels for 19% -> 0%
where the time goes in v3:
time: 135 us
  Pallas kernels  106 us (79%)
  other arithmetic  9.61 us (7%)
  matrix products  8 us (6%)
  between operations  5.52 us (4%)
  local copies, waits for them, and re-layouts  4.55 us (3%)
    pallas_call x1, Pallas kernels, advance(): pl.pallas_call(step_kernel, out_shape=jax.ShapeDtypeStruct(moved.shape, j...  106 us
    unnamed x1, other arithmetic  8.8 us
    dot_general x1, matrix products, body(): first_pass = jnp.einsum('fpqr,kr->fpqk', brick, along_z, precision=HIGH)  4.1 us
    reshape x1, local copies, waits for them, and re-layouts, body(): brick = coarse_bricks.reshape((fields, brick_side, brick_side, brick_depth))  2.92 us
  transfers between devices with their start and end apart: 1, of which 0 were waited for; matrix products, arithmetic and copies ran while one was open for 16% of the time, Pallas kernels for 0%

profile of v3, /device:TPU:0, one launch (start us, length us, event | category | flops | bytes accessed | tf_op | source)
XLA Modules:
  0.0 134.7 jit_solution(2552217294618489496)
XLA Ops:
  0.0 1.3 collective-permute-start
  1.3 8.8 %reduce = f32[235008]{0:T(1024)S(1)} reduce(f32[1,1,1,235008]{3,2,1,0:T(1,128)} %param.8, f32[]{:T(128)} %constant.24), dimensions={0,1,2}, to_apply=%param.8.reduce_sub_computation | reduce | bytes 1880068 | tf_op args[1]
  10.1 0.0 copy-start.2
  10.1 2.9 %reshape.7 = f32[24,12,12,68]{3,2,1,0:T(8,128)} reshape(f32[235008]{0:T(1024)S(1)} %reduce) | data formatting | bytes 1880064 | tf_op jit(solution)/shard_map/reshape | solution.py:572
  13.0 0.0 copy-done.2
  13.0 0.0 copy-start
  13.0 4.1 %fusion.6 = f32[24,12,12,128]{3,0,2,1:T(8,128)S(1)} fusion(f32[128,68,1,1]{0,1,3,2:T(8,128)S(1)} %copy-done.2, f32[24,12,12,68]{3,2,1,0:T(8,128)} %reshape.7), kind=kOutput, calls=%fused_computation.8 | convolution fusion | flops 360972288 | bytes 2744320 | tf_op jit(solution)/shard_map/fpqr,kr->fpqk/dot_general | solution.py:576
  17.1 0.0 copy-done
  17.2 0.6 fusion.20
  21.4 2.1 %fusion.9 = f32[24,12,8,128]{3,2,1,0:T(8,128)S(1)} fusion(f32[24,12,12,128]{3,0,2,1:T(8,128)S(1)} %fusion.6, f32[9,8,12]{2,1,0:T(8,128)} %constant.20.clone, s32[]{:T(128)S(6)} %select_n.17), kind=kOutput, calls=%fused_computation.9 | convolution fusion | flops 42467328 | bytes 2953220 | tf_op jit(solution)/shard_map/fpqk,jq->fpjk/dot_general | solution.py:577
  23.5 0.0 copy-start.3
  23.5 0.0 copy-start.1
  23.5 1.8 %fusion.4 = f32[8,24,8,128]{3,0,2,1:T(8,128)S(1)} fusion(f32[24,12,8,128]{3,2,1,0:T(8,128)S(1)} %fusion.9, f32[9,8,12]{2,1,0:T(8,128)} %constant.20.clone, s32[]{:T(128)S(6)} %select_n.16), kind=kOutput, calls=%fused_computation.6 | convolution fusion | flops 28311552 | bytes 1970180 | tf_op jit(solution)/shard_map/fpjk,ip->fijk/dot_general | solution.py:578
  25.3 0.1 copy.28
  26.6 0.0 copy-done.3
  26.6 0.6 fusion.19
  27.9 0.0 collective-permute-done
  27.9 0.0 copy-done.1
  27.9 0.2 fusion.12.moved_ref
  28.1 105.7 %shard_map.73 = f32[24,8,8,128]{3,2,1,0:T(8,128)S(1)} custom-call(s32[2]{0:T(128)S(1)} %copy-done, s32[1]{0:T(128)} %bitcast.source_ref, f32[24,8,8,128]{3,2,1,0:T(8,128)S(1)} %fusion.12.moved_ref, f32[24,8,8,128]{3,2,1,0:T(8,128)S(1)} %bitcast.28), custom_call_target="tpu_custom_call" | custom-call | tf_op jit(solution)/shard_map/pallas_call | solution.py:503
  133.8 0.9 copy.30
Async XLA Ops:
  0.0 27.9 %collective-permute-start = (f32[24,8,8,128]{3,2,1,0:T(8,128)}, f32[24,8,8,128]{3,2,1,0:T(8,128)S(1)}, u32[]{:S(2)}, u32[]{:S(2)}) collective-permute-start(f32[24,8,8,128]{3,2,1,0:T(8,128)} %param.7), channel_id=1, source_target_pairs={{8,0},{16,8},{24,16},{9,1},{17,9},{25,17},{10,2},{18,10},{26,18},{... | collective-permute-start | bytes 2359304 | tf_op jit(solution)/shard_map/ppermute | solution.py:21
  10.1 2.9 %copy-start.2 = (f32[128,68,1,1]{0,1,3,2:T(8,128)S(1)}, f32[128,68,1,1]{0,1,3,2:T(8,128)}, u32[]{:S(2)}) copy-start(f32[128,68,1,1]{0,1,3,2:T(8,128)} %constant.23) | copy-start | bytes 104452
  13.0 4.1 %copy-start = (s32[2]{0:T(128)S(1)}, s32[2]{0:T(128)}, u32[]{:S(2)}) copy-start(s32[2]{0:T(128)} %shifts_ref.1) | copy-start | bytes 28
  23.5 3.1 %copy-start.3 = (s32[4]{0:T(128)S(1)}, s32[4]{0:T(128)}, u32[]{:S(2)}) copy-start(s32[4]{0:T(128)} %param.10) | copy-start | bytes 52
  23.5 4.4 %copy-start.1 = (f32[24,8,8,128]{3,2,1,0:T(8,128)S(1)}, f32[24,8,8,128]{3,2,1,0:T(8,128)}, u32[]{:S(2)}) copy-start(f32[24,8,8,128]{3,2,1,0:T(8,128)} %param.7) | copy-start | bytes 2359300

commit v4 on v3

--- a/solution.py
+++ b/solution.py
@@ -46,6 +46,7 @@
 def step_kernel(
     shifts_ref, source_ref, moved_ref, filled_ref, out_ref, start_ref, gathered, column, box, zhalo, acc, slopes, ysend, yrecv, csend, crecv, zsend, zcore, zx, zy,
     send_sem, recv_sem, own_send, own_recv, far_send, far_recv, on_send, on_recv, y_send, y_recv,
+    late_send, late_recv, slab_send, slab_recv,
 ):
     fields = start_ref.shape[0]
     portion = fields // PORTIONS
@@ -110,10 +111,11 @@
         for slot in range(2):
             for side in range(2):
                 for j in range(3):
-                    yrecv[slot, side, j, f] = zero
+                    for g in range(fields // 8):
+                        yrecv[slot, side, f, j, pl.ds(8 * g, 8), :] = zero
         return carry
 
-    lax.fori_loop(0, fields, wipe_y, 0)
+    lax.fori_loop(0, 8, wipe_y, 0)
 
     barrier = pltpu.get_barrier_semaphore()
     partner = (place[0] + 1 - 2 * lax.rem(place[0], 2), place[1], place[2])
@@ -200,17 +202,23 @@
             acc[name, x] = value
             box[0, f, 3 + x, pl.ds(8, 8), :] = value
 
-    def message(number, slot):
+    def message(number, slot, piece=0):
         route = ROUTES[number]
+        sent, got = send_sem.at[number], recv_sem.at[slot, number]
         dx, dy, dz = route
         low = lambda side: 1 if side < 0 else 0
         high = lambda side: 0 if side < 0 else 1
         if dx != 0 and dy == 0 and dz == 0:
-            source = box.at[slot, :, pl.ds(3 if dx < 0 else 8, 3), pl.ds(8, 8), :]
-            target = box.at[slot, :, pl.ds(11 if dx < 0 else 0, 3), pl.ds(8, 8), :]
+            first, late = (0, 2) if dx < 0 else (5, 7)
+            start, size = (late, 1) if piece == 1 else (first, 2)
+            source = box.at[slot, :, pl.ds(start + 3, size), pl.ds(8, 8), :]
+            target = box.at[slot, :, pl.ds(start + (11 if dx < 0 else -5), size), pl.ds(8, 8), :]
+            if piece == 1:
+                sent, got = late_send.at[high(dx)], late_recv.at[slot, high(dx)]
         elif dy != 0 and dx == 0 and dz == 0:
-            source = ysend.at[slot, high(dy)]
-            target = yrecv.at[slot, low(dy)]
+            source = ysend.at[slot, high(dy), piece]
+            target = yrecv.at[slot, low(dy), piece]
+            sent, got = slab_send.at[high(dy), piece], slab_recv.at[slot, high(dy), piece]
         elif dz != 0 and dx == 0 and dy == 0:
             source = zsend.at[slot, high(dz)]
             target = zcore.at[slot, low(dz)]
@@ -223,22 +231,58 @@
         else:
             source = zsend.at[slot, high(dz), pl.ds(0, 2)]
             target = zy.at[slot, low(dy), low(dz)]
-        return pltpu.make_async_remote_copy(
-            src_ref=source,
-            dst_ref=target,
-            send_sem=send_sem.at[number],
-            recv_sem=recv_sem.at[slot, number],
-            device_id=peer(route),
-            device_id_type=MESH,
-        )
-
-    def launch(slot, wanted):
+        return remote(source, target, sent, got, peer(route))
+
+    def launch(slot, wanted, piece=0):
         for number, route in enumerate(ROUTES):
             if wanted(route):
 
                 @pl.when(present(route))
                 def _(number=number):
-                    message(number, slot).start()
+                    message(number, slot, piece).start()
+
+    def is_x(route):
+        return route[1] == 0 and route[2] == 0
+
+    def is_y(route):
+        return route[0] == 0 and route[2] == 0
+
+    def finish_all(slot, direction):
+        for number, route in enumerate(ROUTES):
+            ok = present(route if direction == 0 else opposite(route))
+
+            @pl.when(ok)
+            def _(number=number, route=route):
+                def settle(piece):
+                    if direction == 0:
+                        message(number, slot, piece).wait_send()
+                    else:
+                        message(number, slot, piece).wait_recv()
+
+                if is_y(route):
+                    lax.fori_loop(0, 8, lambda x, c: (settle(x), c)[1], 0)
+                else:
+                    settle(0)
+                    if is_x(route):
+                        settle(1)
+
+    def send_slab(slot, x):
+        for side in range(2):
+            for j in range(3):
+                ysend[slot, side, x, j] = box[slot, :, 3 + x, 8 + 5 * side + j, :]
+        launch(slot, is_y, x)
+
+        @pl.when(x == 1)
+        def _():
+            launch(slot, lambda r: is_x(r) and r[0] < 0)
+
+        @pl.when(x == 6)
+        def _():
+            launch(slot, lambda r: is_x(r) and r[0] > 0)
+
+        @pl.when(x == 7)
+        def _():
+            launch(slot, is_x, 1)
 
     def unpacked(from_low, from_high, t):
         return jnp.where(
@@ -249,24 +293,15 @@
 
     def stage(s, carry):
         slot = lax.rem(s, 2)
-        launch(slot, lambda r: r[1] == 0 and r[2] == 0)
-
-        def pack_y(f, c):
-            for j in range(3):
-                ysend[slot, 0, j, f] = box[slot, f, pl.ds(3, 8), 8 + j, :]
-                ysend[slot, 1, j, f] = box[slot, f, pl.ds(3, 8), 13 + j, :]
-            return c
-
-        lax.fori_loop(0, fields, pack_y, 0)
-        launch(slot, lambda r: r[0] == 0 and r[2] == 0)
-        outer = jnp.logical_or(row < 2, row >= 6)
+
         for side in range(2):
-            for f in range(MIXED):
-                csend[slot, side, f] = jnp.where(
-                    outer,
-                    ysend[slot, side, side, f],
-                    pltpu.roll(ysend[slot, side, side + 1, f], 4, axis=0),
-                )
+            for j in range(2):
+                first = 8 if side == 0 else 14
+                for x in (0, 1, 6, 7):
+                    for f in range(MIXED):
+                        csend[slot, side, f, pl.ds((x + 4 * j) % 8, 1), :] = box[
+                            slot, f, 3 + x, pl.ds(first + j, 1), :
+                        ]
         launch(slot, lambda r: r[2] == 0 and r[0] != 0 and r[1] != 0)
 
         def pack_z(g, c):
@@ -286,19 +321,16 @@
         lax.fori_loop(0, groups, pack_z, 0)
         launch(slot, lambda r: r[2] != 0)
 
-        for number, route in enumerate(ROUTES):
-
-            @pl.when(present(opposite(route)))
-            def _(number=number):
-                message(number, slot).wait_recv()
-
-        def spread_y(f, c):
+        finish_all(slot, 1)
+        finish_all(slot, 0)
+
+        def spread_y(x, c):
             for j in range(3):
-                box[slot, f, pl.ds(3, 8), 5 + j, :] = yrecv[slot, 0, j, f]
-                box[slot, f, pl.ds(3, 8), 16 + j, :] = yrecv[slot, 1, j, f]
+                box[slot, :, 3 + x, 5 + j, :] = yrecv[slot, 0, x, j]
+                box[slot, :, 3 + x, 16 + j, :] = yrecv[slot, 1, x, j]
             return c
 
-        lax.fori_loop(0, fields, spread_y, 0)
+        lax.fori_loop(0, 8, spread_y, 0)
         for f in range(MIXED):
             for side, first_row in ((0, 6), (1, 16)):
                 for j in range(2):
@@ -471,17 +503,21 @@
             for n, (i, j) in enumerate(PAIRS):
                 value = ricci[n] - trace if i == j else ricci[n]
                 finish(8 + n, value + free_damp[n])
+
+            @pl.when(s < 3)
+            def _():
+                send_slab(later, x)
+
             return c
 
         lax.fori_loop(0, 8, slab, 0)
-        for number, route in enumerate(ROUTES):
-
-            @pl.when(present(route))
-            def _(number=number):
-                message(number, slot).wait_send()
-
         return carry
 
+    def first_slab(x, carry):
+        send_slab(0, x)
+        return carry
+
+    lax.fori_loop(0, 8, first_slab, 0)
     lax.fori_loop(0, 4, stage, 0)
 
     def hand_out(f, carry):
@@ -514,8 +550,8 @@
             buffer(fields, width + 4, tall),
             buffer(fields, width, height),
             buffer(3, tall),
-            buffer(2, 2, 3, fields, width),
-            buffer(2, 2, 3, fields, width),
+            buffer(2, 2, width, 3, fields),
+            buffer(2, 2, width, 3, fields),
             buffer(2, 2, MIXED, width),
             buffer(2, 2, 2, MIXED, width),
             buffer(2, 2, groups, height),
@@ -532,6 +568,10 @@
             pltpu.SemaphoreType.DMA((PORTIONS,)),
             pltpu.SemaphoreType.DMA,
             pltpu.SemaphoreType.DMA,
+            pltpu.SemaphoreType.DMA((2,)),
+            pltpu.SemaphoreType.DMA((2, 2)),
+            pltpu.SemaphoreType.DMA((2, width)),
+            pltpu.SemaphoreType.DMA((2, 2, width)),
         ],
         compiler_params=pltpu.CompilerParams(
             collective_id=0, has_side_effects=True, vmem_limit_bytes=48 * 1024 * 1024

time: 135 us -> 122 us (0.904)
  Pallas kernels: 106 us -> 92.7 us
    pallas_call x1, Pallas kernels: 106 us -> 92.7 us  [advance(): pl.pallas_call(step_kernel, out_shape=jax.ShapeDtypeStruct(moved.shape, j...]
  transfers between devices with their start and end apart: 1 -> 1, of which waited for: 0 -> 0; matrix products, arithmetic and copies ran while one was open for 16% -> 17% of each run, Pallas kernels for 0% -> 0%
where the time goes in v4:
time: 122 us
  Pallas kernels  92.7 us (76%)
  other arithmetic  9.61 us (8%)
  matrix products  8 us (7%)
  between operations  5.52 us (5%)
  local copies, waits for them, and re-layouts  4.55 us (4%)
  starting transfers between devices  1.28 us (1%)
    pallas_call x1, Pallas kernels, advance(): pl.pallas_call(step_kernel, out_shape=jax.ShapeDtypeStruct(moved.shape, j...  92.7 us
    unnamed x1, other arithmetic  8.8 us
    dot_general x1, matrix products, body(): first_pass = jnp.einsum('fpqr,kr->fpqk', brick, along_z, precision=HIGH)  4.1 us
    reshape x1, local copies, waits for them, and re-layouts, body(): brick = coarse_bricks.reshape((fields, brick_side, brick_side, brick_depth))  2.92 us
  transfers between devices with their start and end apart: 1, of which 0 were waited for; matrix products, arithmetic and copies ran while one was open for 17% of the time, Pallas kernels for 0%

profile of v4, /device:TPU:0, one launch (start us, length us, event | category | flops | bytes accessed | tf_op | source)
XLA Modules:
  0.0 121.7 jit_solution(8700362621160273269)
XLA Ops:
  0.0 1.3 %collective-permute-start = (f32[24,8,8,128]{3,2,1,0:T(8,128)}, f32[24,8,8,128]{3,2,1,0:T(8,128)S(1)}, u32[]{:S(2)}, u32[]{:S(2)}) collective-permute-start(f32[24,8,8,128]{3,2,1,0:T(8,128)} %param.7), channel_id=1, source_target_pairs={{8,0},{16,8},{24,16},{9,1},{17,9},{25,17},{10,2},{18,10},{26,18},{... | collective-permute-start | bytes 2359304 | tf_op jit(solution)/shard_map/ppermute | solution.py:21
  1.3 8.8 %reduce = f32[235008]{0:T(1024)S(1)} reduce(f32[1,1,1,235008]{3,2,1,0:T(1,128)} %param.8, f32[]{:T(128)} %constant.24), dimensions={0,1,2}, to_apply=%param.8.reduce_sub_computation | reduce | bytes 1880068 | tf_op args[1]
  10.1 0.0 copy-start.2
  10.1 2.9 %reshape.7 = f32[24,12,12,68]{3,2,1,0:T(8,128)} reshape(f32[235008]{0:T(1024)S(1)} %reduce) | data formatting | bytes 1880064 | tf_op jit(solution)/shard_map/reshape | solution.py:612
  13.0 0.0 copy-done.2
  13.0 0.0 copy-start
  13.0 4.1 %fusion.6 = f32[24,12,12,128]{3,0,2,1:T(8,128)S(1)} fusion(f32[128,68,1,1]{0,1,3,2:T(8,128)S(1)} %copy-done.2, f32[24,12,12,68]{3,2,1,0:T(8,128)} %reshape.7), kind=kOutput, calls=%fused_computation.8 | convolution fusion | flops 360972288 | bytes 2744320 | tf_op jit(solution)/shard_map/fpqr,kr->fpqk/dot_general | solution.py:616
  17.1 0.0 copy-done
  17.2 0.6 fusion.20
  21.4 2.1 %fusion.9 = f32[24,12,8,128]{3,2,1,0:T(8,128)S(1)} fusion(f32[24,12,12,128]{3,0,2,1:T(8,128)S(1)} %fusion.6, f32[9,8,12]{2,1,0:T(8,128)} %constant.20.clone, s32[]{:T(128)S(6)} %select_n.17), kind=kOutput, calls=%fused_computation.9 | convolution fusion | flops 42467328 | bytes 2953220 | tf_op jit(solution)/shard_map/fpqk,jq->fpjk/dot_general | solution.py:617
  23.5 0.0 copy-start.3
  23.5 0.0 copy-start.1
  23.5 1.8 %fusion.4 = f32[8,24,8,128]{3,0,2,1:T(8,128)S(1)} fusion(f32[24,12,8,128]{3,2,1,0:T(8,128)S(1)} %fusion.9, f32[9,8,12]{2,1,0:T(8,128)} %constant.20.clone, s32[]{:T(128)S(6)} %select_n.16), kind=kOutput, calls=%fused_computation.6 | convolution fusion | flops 28311552 | bytes 1970180 | tf_op jit(solution)/shard_map/fpjk,ip->fijk/dot_general | solution.py:618
  25.3 0.1 copy.28
  26.6 0.0 copy-done.3
  26.6 0.6 fusion.19
  27.9 0.0 collective-permute-done
  27.9 0.0 copy-done.1
  27.9 0.2 fusion.12.moved_ref
  28.1 92.7 %shard_map.73 = f32[24,8,8,128]{3,2,1,0:T(8,128)S(1)} custom-call(s32[2]{0:T(128)S(1)} %copy-done, s32[1]{0:T(128)} %bitcast.source_ref, f32[24,8,8,128]{3,2,1,0:T(8,128)S(1)} %fusion.12.moved_ref, f32[24,8,8,128]{3,2,1,0:T(8,128)S(1)} %bitcast.28), custom_call_target="tpu_custom_call" | custom-call | tf_op jit(solution)/shard_map/pallas_call | solution.py:539
  120.8 0.9 copy.30
Async XLA Ops:
  0.0 27.9 %collective-permute-start = (f32[24,8,8,128]{3,2,1,0:T(8,128)}, f32[24,8,8,128]{3,2,1,0:T(8,128)S(1)}, u32[]{:S(2)}, u32[]{:S(2)}) collective-permute-start(f32[24,8,8,128]{3,2,1,0:T(8,128)} %param.7), channel_id=1, source_target_pairs={{8,0},{16,8},{24,16},{9,1},{17,9},{25,17},{10,2},{18,10},{26,18},{... | collective-permute-start | bytes 2359304 | tf_op jit(solution)/shard_map/ppermute | solution.py:21
  10.1 2.9 %copy-start.2 = (f32[128,68,1,1]{0,1,3,2:T(8,128)S(1)}, f32[128,68,1,1]{0,1,3,2:T(8,128)}, u32[]{:S(2)}) copy-start(f32[128,68,1,1]{0,1,3,2:T(8,128)} %constant.23) | copy-start | bytes 104452
  13.0 4.1 %copy-start = (s32[2]{0:T(128)S(1)}, s32[2]{0:T(128)}, u32[]{:S(2)}) copy-start(s32[2]{0:T(128)} %shifts_ref.1) | copy-start | bytes 28
  23.5 3.1 %copy-start.3 = (s32[4]{0:T(128)S(1)}, s32[4]{0:T(128)}, u32[]{:S(2)}) copy-start(s32[4]{0:T(128)} %param.10) | copy-start | bytes 52
  23.5 4.4 %copy-start.1 = (f32[24,8,8,128]{3,2,1,0:T(8,128)S(1)}, f32[24,8,8,128]{3,2,1,0:T(8,128)}, u32[]{:S(2)}) copy-start(f32[24,8,8,128]{3,2,1,0:T(8,128)} %param.7) | copy-start | bytes 2359300

commit v5 on v4

--- a/solution.py
+++ b/solution.py
@@ -25,7 +25,7 @@
 ORDER = (0, 17, 18, 19, 20, 1, 2, 3, 4, 5, 6, 7, 8, 9, 10, 11, 12, 13, 14, 15, 16, 21, 22, 23)
 PLACE = {field: place for place, field in enumerate(ORDER)}
 MIXED = 5
-PORTIONS = 6
+PORTIONS = 8
 FACES = tuple(
     tuple(side if d == axis else 0 for d in range(3)) for axis in range(3) for side in (-1, 1)
 )
@@ -44,12 +44,11 @@
 
 
 def step_kernel(
-    shifts_ref, source_ref, moved_ref, filled_ref, out_ref, start_ref, gathered, column, box, zhalo, acc, slopes, ysend, yrecv, csend, crecv, zsend, zcore, zx, zy,
+    shifts_ref, source_ref, moved_ref, filled_ref, out_ref, start_ref, gathered, column, pair, box, zhalo, acc, slopes, ysend, yrecv, csend, crecv, zsend, zcore, zx, zy,
     send_sem, recv_sem, own_send, own_recv, far_send, far_recv, on_send, on_recv, y_send, y_recv,
     late_send, late_recv, slab_send, slab_recv,
 ):
     fields = start_ref.shape[0]
-    portion = fields // PORTIONS
     groups = zsend.shape[2]
     counts = tuple(lax.axis_size(name) for name in ("gx", "gy", "gz"))
     place = tuple(lax.axis_index(name) for name in ("gx", "gy", "gz"))
@@ -144,63 +143,41 @@
         )
 
     def far_copy(k):
-        part = pl.ds(k * portion, portion)
+        part = pl.ds(k, 1)
         return remote(
-            filled_ref.at[part], gathered.at[2, part], far_send.at[k], far_recv.at[k], across
+            filled_ref.at[:, part], gathered.at[2, :, part], far_send.at[k], far_recv.at[k], across
         )
 
     def on_copy(k):
-        part = pl.ds(k * portion, portion)
+        part = pl.ds(k, 1)
         return remote(
-            gathered.at[2, part], gathered.at[3, part], on_send.at[k], on_recv.at[k], partner
+            gathered.at[2, :, part], gathered.at[3, :, part], on_send.at[k], on_recv.at[k], partner
         )
 
     own_copy = remote(filled_ref, gathered.at[1], own_send, own_recv, partner)
-    y_copy = remote(
-        moved_ref,
-        column.at[:, :, pl.ds(8, 8), :],
-        y_send,
-        y_recv,
-        (place[0], place[1] - 1, place[2]),
-    )
+    def y_copy(k):
+        return remote(
+            moved_ref.at[:, pl.ds(k, 1)],
+            column.at[:, pl.ds(k, 1), pl.ds(8, 8), :],
+            y_send.at[k],
+            y_recv.at[k],
+            (place[0], place[1] - 1, place[2]),
+        )
 
     @pl.when(place[1] > 0)
     def _():
-        y_copy.start()
+        for k in range(PORTIONS):
+            y_copy(k).start()
 
     for k in range(PORTIONS):
         far_copy(k).start()
     own_copy.start()
     lax.fori_loop(0, fields, keep_own, 0)
-    for k in range(PORTIONS):
-        far_copy(k).wait_recv()
-        on_copy(k).start()
     own_copy.wait()
-    for k in range(PORTIONS):
-        on_copy(k).wait()
-        far_copy(k).wait_send()
-
-    @pl.when(place[1] > 0)
-    def _():
-        y_copy.wait_send()
-
-    @pl.when(place[1] < counts[1] - 1)
-    def _():
-        y_copy.wait_recv()
-
-    chosen = source_ref[0]
+    picked = jnp.zeros((8, 128), jnp.int32) + source_ref[0]
     shift_y = shifts_ref[1]
     row_spot = row + (place[1] * 8 + shifts_ref[1])
     column_entering = row_spot >= 8 * counts[1]
-    for f in range(fields):
-        for x in range(8):
-            x_spot = jnp.zeros((8, 128), jnp.int32) + (place[0] * 8 + x + shifts_ref[0])
-            entering = jnp.logical_or(column_entering, x_spot >= 8 * counts[0])
-            name = ORDER[f]
-            value = jnp.where(entering, gathered[chosen, name, x], column[name, x, pl.ds(shift_y, 8), :])
-            start_ref[name, x] = value
-            acc[name, x] = value
-            box[0, f, 3 + x, pl.ds(8, 8), :] = value
 
     def message(number, slot, piece=0):
         route = ROUTES[number]
@@ -514,10 +491,43 @@
         return carry
 
     def first_slab(x, carry):
+        far_copy(x).wait_recv()
+        on_copy(x).start()
+
+        @pl.when(place[1] < counts[1] - 1)
+        def _():
+            y_copy(x).wait_recv()
+
+        on_copy(x).wait_recv()
+        x_spot = jnp.zeros((8, 128), jnp.int32) + (place[0] * 8 + x + shifts_ref[0])
+        entering = jnp.logical_or(column_entering, x_spot >= 8 * counts[0])
+        for f in range(fields):
+            name = ORDER[f]
+            refill = gathered[0, name, x]
+            for k in range(1, 4):
+                refill = jnp.where(picked == k, gathered[k, name, x], refill)
+            pair[f, pl.ds(0, 8), :] = column[name, x, pl.ds(0, 8), :]
+            pair[f, pl.ds(8, 8), :] = column[name, x, pl.ds(8, 8), :]
+            value = jnp.where(entering, refill, pair[f, pl.ds(shift_y, 8), :])
+            start_ref[name, x] = value
+            acc[name, x] = value
+            box[0, f, 3 + x, pl.ds(8, 8), :] = value
         send_slab(0, x)
         return carry
 
     lax.fori_loop(0, 8, first_slab, 0)
+
+    def settle_sends(x, carry):
+        far_copy(x).wait_send()
+        on_copy(x).wait_send()
+
+        @pl.when(place[1] > 0)
+        def _():
+            y_copy(x).wait_send()
+
+        return carry
+
+    lax.fori_loop(0, PORTIONS, settle_sends, 0)
     lax.fori_loop(0, 4, stage, 0)
 
     def hand_out(f, carry):
@@ -546,6 +556,7 @@
             buffer(fields, width, height),
             buffer(4, fields, width, height),
             buffer(fields, width, 2 * height),
+            buffer(fields, 2 * height),
             buffer(2, fields, width + 6, tall),
             buffer(fields, width + 4, tall),
             buffer(fields, width, height),
@@ -566,8 +577,8 @@
             pltpu.SemaphoreType.DMA((PORTIONS,)),
             pltpu.SemaphoreType.DMA((PORTIONS,)),
             pltpu.SemaphoreType.DMA((PORTIONS,)),
-            pltpu.SemaphoreType.DMA,
-            pltpu.SemaphoreType.DMA,
+            pltpu.SemaphoreType.DMA((PORTIONS,)),
+            pltpu.SemaphoreType.DMA((PORTIONS,)),
             pltpu.SemaphoreType.DMA((2,)),
             pltpu.SemaphoreType.DMA((2, 2)),
             pltpu.SemaphoreType.DMA((2, width)),

time: 122 us -> 118 us (0.967)
  Pallas kernels: 92.7 us -> 88.8 us
    pallas_call x1, Pallas kernels: 92.7 us -> 88.8 us  [advance(): pl.pallas_call(step_kernel, out_shape=jax.ShapeDtypeStruct(moved.shape, j...]
  transfers between devices with their start and end apart: 1 -> 1, of which waited for: 0 -> 0; matrix products, arithmetic and copies ran while one was open for 17% -> 18% of each run, Pallas kernels for 0% -> 0%
where the time goes in v5:
time: 118 us
  Pallas kernels  88.8 us (75%)
  other arithmetic  9.61 us (8%)
  matrix products  8 us (7%)
  between operations  5.52 us (5%)
  local copies, waits for them, and re-layouts  4.55 us (4%)
  starting transfers between devices  1.28 us (1%)
    pallas_call x1, Pallas kernels, advance(): pl.pallas_call(step_kernel, out_shape=jax.ShapeDtypeStruct(moved.shape, j...  88.8 us
    unnamed x1, other arithmetic  8.8 us
    dot_general x1, matrix products, body(): first_pass = jnp.einsum('fpqr,kr->fpqk', brick, along_z, precision=HIGH)  4.1 us
    reshape x1, local copies, waits for them, and re-layouts, body(): brick = coarse_bricks.reshape((fields, brick_side, brick_side, brick_depth))  2.92 us
  transfers between devices with their start and end apart: 1, of which 0 were waited for; matrix products, arithmetic and copies ran while one was open for 18% of the time, Pallas kernels for 0%

profile of v5, /device:TPU:0, one launch (start us, length us, event | category | flops | bytes accessed | tf_op | source)
XLA Modules:
  0.0 117.7 jit_solution(9717159816852102254)
XLA Ops:
  0.0 1.3 %collective-permute-start = (f32[24,8,8,128]{3,2,1,0:T(8,128)}, f32[24,8,8,128]{3,2,1,0:T(8,128)S(1)}, u32[]{:S(2)}, u32[]{:S(2)}) collective-permute-start(f32[24,8,8,128]{3,2,1,0:T(8,128)} %param.7), channel_id=1, source_target_pairs={{8,0},{16,8},{24,16},{9,1},{17,9},{25,17},{10,2},{18,10},{26,18},{... | collective-permute-start | bytes 2359304 | tf_op jit(solution)/shard_map/ppermute | solution.py:21
  1.3 8.8 %reduce = f32[235008]{0:T(1024)S(1)} reduce(f32[1,1,1,235008]{3,2,1,0:T(1,128)} %param.8, f32[]{:T(128)} %constant.24), dimensions={0,1,2}, to_apply=%param.8.reduce_sub_computation | reduce | bytes 1880068 | tf_op args[1]
  10.1 0.0 copy-start.2
  10.1 2.9 %reshape.7 = f32[24,12,12,68]{3,2,1,0:T(8,128)} reshape(f32[235008]{0:T(1024)S(1)} %reduce) | data formatting | bytes 1880064 | tf_op jit(solution)/shard_map/reshape | solution.py:623
  13.0 0.0 copy-done.2
  13.0 0.0 copy-start
  13.0 4.1 %fusion.6 = f32[24,12,12,128]{3,0,2,1:T(8,128)S(1)} fusion(f32[128,68,1,1]{0,1,3,2:T(8,128)S(1)} %copy-done.2, f32[24,12,12,68]{3,2,1,0:T(8,128)} %reshape.7), kind=kOutput, calls=%fused_computation.8 | convolution fusion | flops 360972288 | bytes 2744320 | tf_op jit(solution)/shard_map/fpqr,kr->fpqk/dot_general | solution.py:627
  17.1 0.0 copy-done
  17.2 0.6 fusion.20
  21.4 2.1 %fusion.9 = f32[24,12,8,128]{3,2,1,0:T(8,128)S(1)} fusion(f32[24,12,12,128]{3,0,2,1:T(8,128)S(1)} %fusion.6, f32[9,8,12]{2,1,0:T(8,128)} %constant.20.clone, s32[]{:T(128)S(6)} %select_n.17), kind=kOutput, calls=%fused_computation.9 | convolution fusion | flops 42467328 | bytes 2953220 | tf_op jit(solution)/shard_map/fpqk,jq->fpjk/dot_general | solution.py:628
  23.5 0.0 copy-start.3
  23.5 0.0 copy-start.1
  23.5 1.8 %fusion.4 = f32[8,24,8,128]{3,0,2,1:T(8,128)S(1)} fusion(f32[24,12,8,128]{3,2,1,0:T(8,128)S(1)} %fusion.9, f32[9,8,12]{2,1,0:T(8,128)} %constant.20.clone, s32[]{:T(128)S(6)} %select_n.16), kind=kOutput, calls=%fused_computation.6 | convolution fusion | flops 28311552 | bytes 1970180 | tf_op jit(solution)/shard_map/fpjk,ip->fijk/dot_general | solution.py:629
  25.3 0.1 copy.28
  26.6 0.0 copy-done.3
  26.6 0.6 fusion.19
  27.9 0.0 collective-permute-done
  27.9 0.0 copy-done.1
  27.9 0.2 fusion.12.moved_ref
  28.1 88.8 %shard_map.73 = f32[24,8,8,128]{3,2,1,0:T(8,128)S(1)} custom-call(s32[2]{0:T(128)S(1)} %copy-done, s32[1]{0:T(128)} %bitcast.source_ref, f32[24,8,8,128]{3,2,1,0:T(8,128)S(1)} %fusion.12.moved_ref, f32[24,8,8,128]{3,2,1,0:T(8,128)S(1)} %bitcast.28), custom_call_target="tpu_custom_call" | custom-call | tf_op jit(solution)/shard_map/pallas_call | solution.py:549
  116.9 0.9 copy.30
Async XLA Ops:
  0.0 27.9 %collective-permute-start = (f32[24,8,8,128]{3,2,1,0:T(8,128)}, f32[24,8,8,128]{3,2,1,0:T(8,128)S(1)}, u32[]{:S(2)}, u32[]{:S(2)}) collective-permute-start(f32[24,8,8,128]{3,2,1,0:T(8,128)} %param.7), channel_id=1, source_target_pairs={{8,0},{16,8},{24,16},{9,1},{17,9},{25,17},{10,2},{18,10},{26,18},{... | collective-permute-start | bytes 2359304 | tf_op jit(solution)/shard_map/ppermute | solution.py:21
  10.1 2.9 %copy-start.2 = (f32[128,68,1,1]{0,1,3,2:T(8,128)S(1)}, f32[128,68,1,1]{0,1,3,2:T(8,128)}, u32[]{:S(2)}) copy-start(f32[128,68,1,1]{0,1,3,2:T(8,128)} %constant.23) | copy-start | bytes 104452
  13.0 4.1 %copy-start = (s32[2]{0:T(128)S(1)}, s32[2]{0:T(128)}, u32[]{:S(2)}) copy-start(s32[2]{0:T(128)} %shifts_ref.1) | copy-start | bytes 28
  23.5 3.1 %copy-start.3 = (s32[4]{0:T(128)S(1)}, s32[4]{0:T(128)}, u32[]{:S(2)}) copy-start(s32[4]{0:T(128)} %param.10) | copy-start | bytes 52
  23.5 4.4 %copy-start.1 = (f32[24,8,8,128]{3,2,1,0:T(8,128)S(1)}, f32[24,8,8,128]{3,2,1,0:T(8,128)}, u32[]{:S(2)}) copy-start(f32[24,8,8,128]{3,2,1,0:T(8,128)} %param.7) | copy-start | bytes 2359300
